TPU v7x, 32 devices: a whole 2x2x4 slice. The times are simulated.
32 devices in a mesh: groups: 2 (over y), ctx: 4 (over z), head: 4 (over x, core).
Axes of the slice: x: 2, y: 2, z: 4, core: 2. Of those that a mesh axis runs over, the one named last changes fastest.
Arguments:
- queries: bfloat16 [4096, 4096], P(('groups', 'ctx'), 'head'), parts along dimension 0, may hold values from -40 to 40
- keys: bfloat16 [4096, 4096], P(('groups', 'ctx'), 'head'), parts along dimension 0, may hold values from -4 to 4
- values: bfloat16 [4096, 4096], P(('groups', 'ctx'), 'head'), parts along dimension 0, may hold values from -40 to 40
- log_decay: bfloat16 [4096, 32], P(('groups', 'ctx'), 'head'), parts along dimension 0, may hold values from -1.6 to 0
- arrival_positions: int32 [4096], P(('groups', 'ctx')), parts along dimension 0, may hold values from 0 to 2047, as said below
- prompt_lengths: int32 [8], P('groups'), parts along dimension 0, may hold values from 1 to 1024, 2048 in all
- norm_gain: float32 [4096], P('head'), may hold values from 0.5 to 2
- out_weight: bfloat16 [4096, 6144], P(None, 'head'), may hold values from -0.09375 to 0.09375
Outputs:
- layer_out: bfloat16 [4096, 6144], P(('groups', 'ctx'), 'head'), parts along dimension 0
There are 2 independent parts, one for each index of `groups`. A program takes and returns all parts, laid end to end along the dimension named above; an argument that names none is the same for every part. Nothing has to cross between parts.
Inputs may be any that keep to these rules, and one draw needn't show every extreme that they name: `arrival_positions`: each packed position appears once. The rows that one arrival device holds of one owner are one run of consecutive positions, of 64 or 192 rows, and every arrival device holds such a run of every owner. `prompt_lengths`: they sum to 2048; the longest is exactly 1024.
All inputs are finite; a program needn't handle non-finite values.
Results may differ from a plain program's by a relative error of at most 0.013.
Values may be sent and summed in bfloat16 or wider, within the bound.
A program may use at most 64 MiB of HBM per device.

v0:
```python
import functools

import jax
import jax.numpy as jnp
from jax import lax
from jax.experimental import pallas as pl
from jax.experimental.pallas import tpu as pltpu
from jax.sharding import PartitionSpec as P


def split_terms(source):
    upper_part = source.astype(jnp.bfloat16)
    lower_part = (source - upper_part.astype(jnp.float32)).astype(jnp.bfloat16)
    return (upper_part, lower_part)


def paired_einsum(form, wide_operand, narrow_operand, wide_first):
    upper_part, lower_part = split_terms(wide_operand)
    if wide_first:
        return jnp.einsum(
            form, upper_part, narrow_operand, preferred_element_type=jnp.float32
        ) + jnp.einsum(form, lower_part, narrow_operand, preferred_element_type=jnp.float32)
    return jnp.einsum(
        form, narrow_operand, upper_part, preferred_element_type=jnp.float32
    ) + jnp.einsum(form, narrow_operand, lower_part, preferred_element_type=jnp.float32)


def block_terms(run_state, last_seg, block_q, block_k, block_v, block_cum, block_seg):
    linked = block_seg == last_seg
    reach_back = jnp.where(linked[:, None], jnp.exp(block_cum), 0.0)
    earlier = paired_einsum("thd,hde->the", run_state, block_q, False) * reach_back[:, :, None]
    block_rows = block_seg.shape[0]
    order_ok = jnp.arange(block_rows)[:, None] >= jnp.arange(block_rows)[None, :]
    allowed = order_ok & (block_seg[:, None] == block_seg[None, :])
    by_head = block_cum.T
    spread = by_head[:, :, None] - by_head[:, None, :]
    decay_table = jnp.where(allowed[None], jnp.exp(jnp.where(allowed[None], spread, 0.0)), 0.0)
    scores = jnp.einsum("thd,shd->hts", block_q, block_k, preferred_element_type=jnp.float32)
    inside = paired_einsum("hts,shd->thd", scores * decay_table, block_v, True)
    end_seg = block_seg[-1]
    toward = jnp.where(
        (block_seg == end_seg)[:, None], jnp.exp(block_cum[-1][None, :] - block_cum), 0.0
    )
    local_state = paired_einsum(
        "shd,she->hde", block_k.astype(jnp.float32) * toward[:, :, None], block_v, True
    )
    keep_factor = jnp.where(jnp.all(linked), jnp.exp(block_cum[-1]), 0.0)
    new_state = keep_factor[:, None, None] * run_state + local_state
    return (earlier + inside, new_state)


def attend(own_q, own_k, own_v, cumulative, segment, run_state, last_seg):
    block_out, run_state = block_terms(
        run_state, last_seg, own_q, own_k, own_v, cumulative, segment
    )
    return (block_out, run_state)


def carried_state(factor, end_state):
    owner_count = lax.axis_size("ctx")
    my_index = lax.axis_index("ctx")
    factors, states = (
        lax.all_gather(factor[None].astype(jnp.bfloat16), "ctx", axis=0, tiled=True).astype(
            jnp.float32
        ),
        lax.all_gather(end_state[None].astype(jnp.bfloat16), "ctx", axis=0, tiled=True).astype(
            jnp.float32
        ),
    )
    index_line = jnp.arange(owner_count)
    between = (index_line[None, :] > index_line[:, None]) & (index_line[None, :] < my_index)
    chain_weights = jnp.prod(jnp.where(between[:, :, None], factors[None, :, :], 1.0), axis=1)
    chain_weights = chain_weights * (index_line < my_index)[:, None].astype(jnp.float32)
    return jnp.einsum("nh,nhde->hde", chain_weights, states, precision=lax.Precision.HIGHEST)


def exchange_form(
    queries, keys, values, log_decay, arrival_positions, prompt_lengths, norm_gain, out_weight
):
    row_count = queries.shape[0]
    heads_here = log_decay.shape[1]
    head_width = queries.shape[1] // heads_here
    owner_count = lax.axis_size("ctx")
    my_index = lax.axis_index("ctx")
    capacity = 3 * (row_count // (2 * owner_count))
    slot_total = owner_count * capacity
    every_position = lax.all_gather(arrival_positions, "ctx", axis=0, tiled=True)
    target = arrival_positions // row_count
    hit_table = (target[:, None] == jnp.arange(owner_count)[None, :]).astype(jnp.int32)
    slot_index = jnp.sum((jnp.cumsum(hit_table, axis=0) - 1) * hit_table, axis=1)
    send_slot = target * capacity + slot_index
    send_onehot = (jnp.arange(slot_total)[:, None] == send_slot[None, :]).astype(jnp.bfloat16)

    def pack_rows(source):
        packed = jnp.dot(send_onehot, source, preferred_element_type=jnp.float32).astype(
            source.dtype
        )
        return packed.reshape(owner_count, capacity, source.shape[1])

    arrived = (
        lax.all_to_all(pack_rows(queries), "ctx", split_axis=0, concat_axis=0, tiled=True),
        lax.all_to_all(pack_rows(keys), "ctx", split_axis=0, concat_axis=0, tiled=True),
        lax.all_to_all(pack_rows(values), "ctx", split_axis=0, concat_axis=0, tiled=True),
        lax.all_to_all(pack_rows(log_decay), "ctx", split_axis=0, concat_axis=0, tiled=True),
    )
    layout = every_position.reshape(owner_count, row_count)
    own_rows = layout // row_count == my_index
    rank_index = jnp.cumsum(own_rows.astype(jnp.int32), axis=1) - 1
    source_slot = (jnp.arange(owner_count)[:, None] * capacity + rank_index).reshape(-1)
    wanted = my_index * row_count + jnp.arange(row_count, dtype=jnp.int32)
    matches = every_position[None, :] == wanted[:, None]
    slot_of_row = jnp.sum(jnp.where(matches, source_slot[None, :], 0), axis=1)
    receive_onehot = (slot_of_row[:, None] == jnp.arange(slot_total)[None, :]).astype(jnp.bfloat16)

    def unpack_rows(buffer):
        flat_buffer = buffer.reshape(slot_total, buffer.shape[2])
        return jnp.dot(receive_onehot, flat_buffer, preferred_element_type=jnp.float32).astype(
            buffer.dtype
        )

    own_q = unpack_rows(arrived[0]).reshape(row_count, heads_here, head_width)
    own_k = unpack_rows(arrived[1]).reshape(row_count, heads_here, head_width)
    own_v = unpack_rows(arrived[2]).reshape(row_count, heads_here, head_width)
    cumulative = jnp.cumsum(unpack_rows(arrived[3]).astype(jnp.float32), axis=0)
    positions = my_index * row_count + jnp.arange(row_count, dtype=jnp.int32)
    prompt_ends = jnp.cumsum(prompt_lengths)[:-1]
    segment = jnp.sum((positions[:, None] >= prompt_ends[None, :]).astype(jnp.int32), axis=1)
    opens_prompt = (positions[0] == 0) | jnp.any(positions[0] == prompt_ends)
    through = jnp.logical_not(opens_prompt) & jnp.all(segment == segment[0])
    factor = jnp.where(through, jnp.exp(cumulative[-1]), 0.0)
    entry_seg = jnp.where(opens_prompt, -1, segment[0])
    empty_state = jnp.zeros((heads_here, head_width, head_width), jnp.float32)
    attention, end_state = attend(
        own_q, own_k, own_v, cumulative, segment, empty_state, jnp.int32(-1)
    )
    incoming = carried_state(factor, end_state)
    reach_back = jnp.where((segment == entry_seg)[:, None], jnp.exp(cumulative), 0.0)
    attention = (
        attention + paired_einsum("thd,hde->the", incoming, own_q, False) * reach_back[:, :, None]
    )
    inv_scale = lax.rsqrt(jnp.mean(attention * attention, axis=-1, keepdims=True) + 1e-06)
    normed = (attention * inv_scale * norm_gain.reshape(heads_here, head_width)).astype(
        jnp.bfloat16
    )
    normed = normed.reshape(row_count, heads_here * head_width)
    projected = jnp.dot(
        lax.all_gather(normed, "head", axis=1, tiled=True),
        out_weight,
        preferred_element_type=jnp.float32,
    )
    return projected.astype(jnp.bfloat16)


CHUNK = 256
MESH = pl.DeviceIdType.MESH
NT = (((1,), (1,)), ((), ()))
TN = (((0,), (0,)), ((), ()))


def dot32(left, right, dims=(((1,), (0,)), ((), ()))):
    return lax.dot_general(left, right, dims, preferred_element_type=jnp.float32)


def fused_kernel(
    owners,
    rows,
    lanes,
    prompts,
    lengths_ref,
    meta_ref,
    gain_ref,
    q_ref,
    k_ref,
    v_ref,
    w_ref,
    out_ref,
    meta_buf,
    in_buf,
    place,
    cum_col,
    cum_row,
    state,
    normed,
    gathered,
    weights,
    total,
    meta_l,
    meta_s,
    meta_r,
    in_l,
    in_s,
    in_r,
    w_l,
    out_l,
    out_s,
    out_r,
    sib_s,
    sib_r,
    cross_s,
    cross_r,
    relay_s,
    relay_r,
):
    me = lax.axis_index("ctx")
    my_head = lax.axis_index("head")
    sibling = my_head + 1 - 2 * lax.rem(my_head, 2)
    cross = lax.rem(my_head + 2, 4)
    diagonal = lax.rem(sibling + 2, 4)
    tokens = owners * rows
    peers = [lax.rem(me + step, owners) for step in range(owners)]
    sources = (q_ref, k_ref, v_ref)

    barrier = pltpu.get_barrier_semaphore()
    for peer in peers[1:]:
        pl.semaphore_signal(barrier, inc=1, device_id={"ctx": peer}, device_id_type=MESH)
    for peer in (sibling, cross):
        pl.semaphore_signal(barrier, inc=1, device_id={"head": peer}, device_id_type=MESH)
    pl.semaphore_wait(barrier, owners + 1)

    def token_rows(index):
        return pl.ds(pl.multiple_of(index * rows, rows), rows)

    def meta_send(peer, source):
        return pltpu.make_async_remote_copy(
            src_ref=meta_ref.at[peer],
            dst_ref=meta_buf.at[:, token_rows(source)],
            send_sem=meta_s.at[peer],
            recv_sem=meta_r.at[source],
            device_id={"ctx": peer},
            device_id_type=MESH,
        )

    def lane_block(index):
        return pl.ds(pl.multiple_of(index * lanes, lanes), lanes)

    def in_send(j, a, peer, source):
        return pltpu.make_async_remote_copy(
            src_ref=sources[a].at[:, lane_block(peer * 2 + j)],
            dst_ref=in_buf.at[j, token_rows(source), pl.ds(a * lanes, lanes)],
            send_sem=in_s.at[j, a, peer],
            recv_sem=in_r.at[j, a, source],
            device_id={"ctx": peer},
            device_id_type=MESH,
        )

    def in_local(j, a):
        return pltpu.make_async_copy(
            sources[a].at[:, lane_block(me * 2 + j)],
            in_buf.at[j, token_rows(me), pl.ds(a * lanes, lanes)],
            in_l.at[j, a],
        )

    def piece(j, head_index, source):
        return gathered.at[j, :, lane_block(head_index * owners + source)]

    def out_send(j, owner, source):
        return pltpu.make_async_remote_copy(
            src_ref=normed.at[j, token_rows(owner)],
            dst_ref=piece(j, my_head, source),
            send_sem=out_s.at[j, owner],
            recv_sem=out_r.at[j, source],
            device_id={"ctx": owner},
            device_id_type=MESH,
        )

    def out_local(j):
        return pltpu.make_async_copy(
            normed.at[j, token_rows(me)], piece(j, my_head, me), out_l.at[j]
        )

    def head_send(j, source, head_index, target, send, recv):
        return pltpu.make_async_remote_copy(
            src_ref=piece(j, head_index, source),
            dst_ref=piece(j, head_index, source),
            send_sem=send.at[j, source],
            recv_sem=recv.at[j, source],
            device_id={"head": target},
            device_id_type=MESH,
        )

    def weight_load(j):
        return pltpu.make_async_copy(w_ref.at[:, j], weights.at[j], w_l.at[j])

    for peer in peers[1:]:
        meta_send(peer, me).start()
    meta_local = pltpu.make_async_copy(
        meta_ref.at[me], meta_buf.at[:, token_rows(me)], meta_l.at[0]
    )
    meta_local.start()
    for j in range(2):
        for a in range(3):
            for peer in peers[1:]:
                in_send(j, a, peer, me).start()
    for j in range(2):
        for a in range(3):
            in_local(j, a).start()
    for j in range(2):
        weight_load(j).start()

    meta_local.wait()
    for peer in peers[1:]:
        meta_send(me, peer).wait_recv()

    line_col = lax.broadcasted_iota(jnp.int32, (CHUNK, CHUNK), 0)
    line_row = lax.broadcasted_iota(jnp.int32, (CHUNK, CHUNK), 1)
    earlier_mask = line_col >= line_row

    def prepare(index, carry):
        start = pl.multiple_of(index * CHUNK, CHUNK)
        held = meta_buf[...]
        wanted = (lax.broadcasted_iota(jnp.int32, (CHUNK, 1), 0) + start).astype(jnp.float32)
        hits = jnp.where(held[2:3, :] == wanted, 1.0, 0.0).astype(jnp.bfloat16)
        place[pl.ds(start, CHUNK), :] = hits
        decay = held.astype(jnp.bfloat16)
        lower = jnp.where(earlier_mask, 1.0, 0.0).astype(jnp.bfloat16)
        decay_col = dot32(hits, decay, NT).astype(jnp.bfloat16)
        decay_row = dot32(decay, hits, NT).astype(jnp.bfloat16)
        cum_col[pl.ds(start, CHUNK), :] = dot32(lower, decay_col)
        cum_row[:, pl.ds(start, CHUNK)] = dot32(decay_row, lower, NT)
        return carry

    lax.fori_loop(0, tokens // CHUNK, prepare, 0)

    ends = []
    running = lengths_ref[0]
    for index in range(1, prompts):
        ends.append(running)
        running = running + lengths_ref[index]

    def segment_of(position):
        found = jnp.zeros_like(position)
        for end in ends:
            found = found + jnp.where(position >= end, 1, 0)
        return found

    def chunk(j, start):
        rows_here = pl.ds(start, CHUNK)
        packed = dot32(place[rows_here, :], in_buf[j]).astype(jnp.bfloat16)
        query = packed[:, :lanes]
        key = packed[:, lanes : 2 * lanes]
        value = packed[:, 2 * lanes :]
        col = cum_col[rows_here, :][:, j : j + 1]
        row = cum_row[:, rows_here][j : j + 1, :]
        last = col[CHUNK - 1 :, :]
        seg_col = segment_of(start + lax.broadcasted_iota(jnp.int32, (CHUNK, 1), 0))
        seg_row = segment_of(start + lax.broadcasted_iota(jnp.int32, (1, CHUNK), 1))
        seg_end = segment_of(start + jnp.full((1, 1), CHUNK - 1, jnp.int32))
        before = start + jnp.full((1, 1), -1, jnp.int32)
        seg_before = jnp.where(before < 0, -1, segment_of(before))
        allowed = earlier_mask & (seg_col == seg_row)
        table = jnp.exp(jnp.where(allowed, col - row, -1e30))
        scores = dot32(query, key, NT) * table
        held = state[...]
        reach = jnp.where(seg_col == seg_before, jnp.exp(col), 0.0)
        result = dot32(scores.astype(jnp.bfloat16), value)
        result = result + dot32(query, held.astype(jnp.bfloat16)) * reach
        toward = jnp.where(seg_col == seg_end, jnp.exp(last - col), 0.0)
        weighted = (key.astype(jnp.float32) * toward).astype(jnp.bfloat16)
        keep = jnp.where(seg_end == seg_before, jnp.exp(last), 0.0)
        state[...] = keep * held + dot32(weighted, value, TN)
        scale = lax.rsqrt(jnp.mean(result * result, axis=-1, keepdims=True) + 1e-06)
        gain = gain_ref[pl.ds(me * 2 + j, 1), :]
        normed[j, rows_here, :] = (result * scale * gain).astype(jnp.bfloat16)

    def forward(j, source):
        head_send(j, source, my_head, cross, cross_s, cross_r).start()
        head_send(j, source, my_head, sibling, sib_s, sib_r).start()

    def arrive(j, source):
        out_send(j, me, source).wait_recv()
        forward(j, source)

    def relay(j, source):
        head_send(j, source, cross, cross, cross_s, cross_r).wait_recv()
        head_send(j, source, cross, sibling, relay_s, relay_r).start()

    for j in range(2):
        for a in range(3):
            in_local(j, a).wait()
            for peer in peers[1:]:
                in_send(j, a, me, peer).wait_recv()
        state[...] = jnp.zeros_like(state)

        def owner_block(owner, carry):
            for part in range(rows // CHUNK):
                chunk(j, pl.multiple_of(owner * rows + part * CHUNK, CHUNK))
            return carry

        lax.fori_loop(0, owners, owner_block, 0)
        out_local(j).start()
        for peer in peers[1:]:
            out_send(j, peer, me).start()
        out_local(j).wait()
        forward(j, me)

    def collect(j):
        for source in peers:
            head_send(j, source, sibling, sibling, sib_s, sib_r).wait_recv()
            head_send(j, source, diagonal, sibling, relay_s, relay_r).wait_recv()

    width = out_ref.shape[1]
    tile = 256
    depth = owners * lanes

    def project(j, groups, first, final):
        def columns_of(index, carry):
            columns = pl.ds(pl.multiple_of(index * tile, tile), tile)
            summed = None if first else total[:, columns]
            for group in groups:
                left = gathered[j, :, pl.ds(pl.multiple_of(group * depth, depth), depth)]
                right = weights[j, pl.ds(group * owners, owners), :, columns]
                term = dot32(left, right.reshape(depth, tile))
                summed = term if summed is None else summed + term
            if final:
                out_ref[:, columns] = summed.astype(out_ref.dtype)
            else:
                total[:, columns] = summed
            return carry

        lax.fori_loop(0, width // tile, columns_of, 0)

    relay(0, me)
    for peer in peers[1:]:
        arrive(0, peer)
    relay(1, me)
    weight_load(0).wait()
    weight_load(1).wait()
    for peer in peers[1:]:
        relay(0, peer)
        arrive(1, peer)
    project(0, (my_head, cross), True, False)
    relay(1, peers[1])
    collect(0)
    project(0, (sibling, diagonal), False, False)
    for peer in peers[2:]:
        relay(1, peer)
    project(1, (my_head, cross), False, False)
    collect(1)
    project(1, (sibling, diagonal), False, True)

    for peer in peers[1:]:
        meta_send(peer, me).wait_send()
    for j in range(2):
        for peer in peers[1:]:
            for a in range(3):
                in_send(j, a, peer, me).wait_send()
            out_send(j, peer, me).wait_send()
        for source in peers:
            head_send(j, source, my_head, cross, cross_s, cross_r).wait_send()
            head_send(j, source, my_head, sibling, sib_s, sib_r).wait_send()
            head_send(j, source, cross, sibling, relay_s, relay_r).wait_send()


def fused_form(
    queries, keys, values, log_decay, arrival_positions, prompt_lengths, norm_gain, out_weight
):
    rows = queries.shape[0]
    heads_here = log_decay.shape[1]
    lanes = queries.shape[1] // heads_here
    owners = lax.axis_size("ctx")
    tokens = owners * rows
    features, width = out_weight.shape
    decay = log_decay.astype(jnp.float32).T.reshape(owners, 2, rows)
    where = jnp.broadcast_to(arrival_positions.astype(jnp.float32), (owners, 1, rows))
    meta = jnp.concatenate([decay, where, jnp.zeros((owners, 5, rows), jnp.float32)], axis=1)
    gain = norm_gain.reshape(heads_here, lanes)
    stacked = out_weight.reshape(features // (2 * lanes), 2, lanes, width)
    vmem = pl.BlockSpec(memory_space=pltpu.VMEM)
    anywhere = pl.BlockSpec(memory_space=pl.ANY)
    dma = pltpu.SemaphoreType.DMA
    return pl.pallas_call(
        functools.partial(fused_kernel, owners, rows, lanes, prompt_lengths.shape[0]),
        out_shape=jax.ShapeDtypeStruct((rows, width), jnp.bfloat16),
        in_specs=[
            pl.BlockSpec(memory_space=pltpu.SMEM),
            vmem,
            vmem,
            anywhere,
            anywhere,
            anywhere,
            anywhere,
        ],
        out_specs=vmem,
        scratch_shapes=[
            pltpu.VMEM((8, tokens), jnp.float32),
            pltpu.VMEM((2, tokens, 3 * lanes), jnp.bfloat16),
            pltpu.VMEM((tokens, tokens), jnp.bfloat16),
            pltpu.VMEM((tokens, 8), jnp.float32),
            pltpu.VMEM((8, tokens), jnp.float32),
            pltpu.VMEM((lanes, lanes), jnp.float32),
            pltpu.VMEM((2, tokens, lanes), jnp.bfloat16),
            pltpu.VMEM((2, rows, features // 2), jnp.bfloat16),
            pltpu.VMEM((2, features // (2 * lanes), lanes, width), jnp.bfloat16),
            pltpu.VMEM((rows, width), jnp.float32),
            dma((1,)),
            dma((owners,)),
            dma((owners,)),
            dma((2, 3)),
            dma((2, 3, owners)),
            dma((2, 3, owners)),
            dma((2,)),
            dma((2,)),
            dma((2, owners)),
            dma((2, owners)),
            dma((2, owners)),
            dma((2, owners)),
            dma((2, owners)),
            dma((2, owners)),
            dma((2, owners)),
            dma((2, owners)),
        ],
        compiler_params=pltpu.CompilerParams(
            collective_id=0, has_side_effects=True, vmem_limit_bytes=56 * 1024 * 1024
        ),
    )(prompt_lengths, meta, gain, queries, keys, values, stacked)


def local(*arguments):
    queries, log_decay = arguments[0], arguments[3]
    fits = (
        log_decay.shape[1] == 2 * lax.axis_size("ctx")
        and lax.axis_size("head") == 4
        and queries.shape[0] % CHUNK == 0
        and queries.shape[1] == 128 * log_decay.shape[1]
    )
    return (fused_form if fits else exchange_form)(*arguments)


def solution(mesh):
    return jax.shard_map(
        local,
        mesh=mesh,
        in_specs=(
            P(("groups", "ctx"), "head"),
            P(("groups", "ctx"), "head"),
            P(("groups", "ctx"), "head"),
            P(("groups", "ctx"), "head"),
            P(("groups", "ctx")),
            P("groups"),
            P("head"),
            P(None, "head"),
        ),
        out_specs=P(("groups", "ctx"), "head"),
        check_vma=False,
    )
```

profile of v0, /device:TPU:8, one launch (start us, length us, event | category | flops | bytes accessed | tf_op | source)
XLA Modules:
  0.0 120.8 jit_solution(15690179165465187287)
XLA Ops:
  0.0 0.1 pad.2.clone
  0.1 0.7 convert_element_type.4
  0.8 0.7 convert_bitcast_fusion
  1.5 0.7 maximum_maximum_fusion.meta_ref
  2.2 116.0 %shard_map.82 = bf16[512,1536]{1,0:T(8,128)(2,1)} custom-call(s32[4]{0:T(128)} %lengths_ref.1, f32[4,8,512]{2,1,0:T(8,128)} %maximum_maximum_fusion.meta_ref, f32[8,128]{1,0:T(8,128)} %bitcast.5, bf16[512,1024]{1,0:T(8,128)(2,1)} %q_ref.1, bf16[512,1024]{1,0:T(8,128)(2,1)} %k_ref.1, bf16[512,1024]{1,0:T(8,128)(2,1)} %v_ref.1, bf16[16,2,128,1536]{3,2,1,0:T(8,128)(2,1)} %bitcast.4), custom_call_target="tpu_custom_call" | custom-call | tf_op jit(solution)/shard_map/pallas_call | solution.py:471
  118.2 2.7 %copy.10 = bf16[512,1536]{1,0:T(8,128)(2,1)} copy(bf16[512,1536]{1,0:T(8,128)(2,1)} %shard_map.82) | data formatting | bytes 3145728
  (3 shorter events, 0.0 us)
where the time goes:
time: 121 us
  Pallas kernels  116 us (96%)
  local copies, waits for them, and re-layouts  2.76 us (2%)
  other arithmetic  2.09 us (2%)
    pallas_call x1, Pallas kernels, fused_form(): pl.pallas_call(functools.partial(fused_kernel, owners, rows, lanes, promp...  116 us
    unnamed x1, local copies, waits for them, and re-layouts  2.65 us

commit v1 on v0

v1 whole, which is shorter than its diff:
```python
import functools

import jax
import jax.numpy as jnp
from jax import lax
from jax.experimental import pallas as pl
from jax.experimental.pallas import tpu as pltpu
from jax.sharding import PartitionSpec as P


def split_terms(source):
    upper_part = source.astype(jnp.bfloat16)
    lower_part = (source - upper_part.astype(jnp.float32)).astype(jnp.bfloat16)
    return (upper_part, lower_part)


def paired_einsum(form, wide_operand, narrow_operand, wide_first):
    upper_part, lower_part = split_terms(wide_operand)
    if wide_first:
        return jnp.einsum(
            form, upper_part, narrow_operand, preferred_element_type=jnp.float32
        ) + jnp.einsum(form, lower_part, narrow_operand, preferred_element_type=jnp.float32)
    return jnp.einsum(
        form, narrow_operand, upper_part, preferred_element_type=jnp.float32
    ) + jnp.einsum(form, narrow_operand, lower_part, preferred_element_type=jnp.float32)


def block_terms(run_state, last_seg, block_q, block_k, block_v, block_cum, block_seg):
    linked = block_seg == last_seg
    reach_back = jnp.where(linked[:, None], jnp.exp(block_cum), 0.0)
    earlier = paired_einsum("thd,hde->the", run_state, block_q, False) * reach_back[:, :, None]
    block_rows = block_seg.shape[0]
    order_ok = jnp.arange(block_rows)[:, None] >= jnp.arange(block_rows)[None, :]
    allowed = order_ok & (block_seg[:, None] == block_seg[None, :])
    by_head = block_cum.T
    spread = by_head[:, :, None] - by_head[:, None, :]
    decay_table = jnp.where(allowed[None], jnp.exp(jnp.where(allowed[None], spread, 0.0)), 0.0)
    scores = jnp.einsum("thd,shd->hts", block_q, block_k, preferred_element_type=jnp.float32)
    inside = paired_einsum("hts,shd->thd", scores * decay_table, block_v, True)
    end_seg = block_seg[-1]
    toward = jnp.where(
        (block_seg == end_seg)[:, None], jnp.exp(block_cum[-1][None, :] - block_cum), 0.0
    )
    local_state = paired_einsum(
        "shd,she->hde", block_k.astype(jnp.float32) * toward[:, :, None], block_v, True
    )
    keep_factor = jnp.where(jnp.all(linked), jnp.exp(block_cum[-1]), 0.0)
    new_state = keep_factor[:, None, None] * run_state + local_state
    return (earlier + inside, new_state)


def attend(own_q, own_k, own_v, cumulative, segment, run_state, last_seg):
    block_out, run_state = block_terms(
        run_state, last_seg, own_q, own_k, own_v, cumulative, segment
    )
    return (block_out, run_state)


def carried_state(factor, end_state):
    owner_count = lax.axis_size("ctx")
    my_index = lax.axis_index("ctx")
    factors, states = (
        lax.all_gather(factor[None].astype(jnp.bfloat16), "ctx", axis=0, tiled=True).astype(
            jnp.float32
        ),
        lax.all_gather(end_state[None].astype(jnp.bfloat16), "ctx", axis=0, tiled=True).astype(
            jnp.float32
        ),
    )
    index_line = jnp.arange(owner_count)
    between = (index_line[None, :] > index_line[:, None]) & (index_line[None, :] < my_index)
    chain_weights = jnp.prod(jnp.where(between[:, :, None], factors[None, :, :], 1.0), axis=1)
    chain_weights = chain_weights * (index_line < my_index)[:, None].astype(jnp.float32)
    return jnp.einsum("nh,nhde->hde", chain_weights, states, precision=lax.Precision.HIGHEST)


def exchange_form(
    queries, keys, values, log_decay, arrival_positions, prompt_lengths, norm_gain, out_weight
):
    row_count = queries.shape[0]
    heads_here = log_decay.shape[1]
    head_width = queries.shape[1] // heads_here
    owner_count = lax.axis_size("ctx")
    my_index = lax.axis_index("ctx")
    capacity = 3 * (row_count // (2 * owner_count))
    slot_total = owner_count * capacity
    every_position = lax.all_gather(arrival_positions, "ctx", axis=0, tiled=True)
    target = arrival_positions // row_count
    hit_table = (target[:, None] == jnp.arange(owner_count)[None, :]).astype(jnp.int32)
    slot_index = jnp.sum((jnp.cumsum(hit_table, axis=0) - 1) * hit_table, axis=1)
    send_slot = target * capacity + slot_index
    send_onehot = (jnp.arange(slot_total)[:, None] == send_slot[None, :]).astype(jnp.bfloat16)

    def pack_rows(source):
        packed = jnp.dot(send_onehot, source, preferred_element_type=jnp.float32).astype(
            source.dtype
        )
        return packed.reshape(owner_count, capacity, source.shape[1])

    arrived = (
        lax.all_to_all(pack_rows(queries), "ctx", split_axis=0, concat_axis=0, tiled=True),
        lax.all_to_all(pack_rows(keys), "ctx", split_axis=0, concat_axis=0, tiled=True),
        lax.all_to_all(pack_rows(values), "ctx", split_axis=0, concat_axis=0, tiled=True),
        lax.all_to_all(pack_rows(log_decay), "ctx", split_axis=0, concat_axis=0, tiled=True),
    )
    layout = every_position.reshape(owner_count, row_count)
    own_rows = layout // row_count == my_index
    rank_index = jnp.cumsum(own_rows.astype(jnp.int32), axis=1) - 1
    source_slot = (jnp.arange(owner_count)[:, None] * capacity + rank_index).reshape(-1)
    wanted = my_index * row_count + jnp.arange(row_count, dtype=jnp.int32)
    matches = every_position[None, :] == wanted[:, None]
    slot_of_row = jnp.sum(jnp.where(matches, source_slot[None, :], 0), axis=1)
    receive_onehot = (slot_of_row[:, None] == jnp.arange(slot_total)[None, :]).astype(jnp.bfloat16)

    def unpack_rows(buffer):
        flat_buffer = buffer.reshape(slot_total, buffer.shape[2])
        return jnp.dot(receive_onehot, flat_buffer, preferred_element_type=jnp.float32).astype(
            buffer.dtype
        )

    own_q = unpack_rows(arrived[0]).reshape(row_count, heads_here, head_width)
    own_k = unpack_rows(arrived[1]).reshape(row_count, heads_here, head_width)
    own_v = unpack_rows(arrived[2]).reshape(row_count, heads_here, head_width)
    cumulative = jnp.cumsum(unpack_rows(arrived[3]).astype(jnp.float32), axis=0)
    positions = my_index * row_count + jnp.arange(row_count, dtype=jnp.int32)
    prompt_ends = jnp.cumsum(prompt_lengths)[:-1]
    segment = jnp.sum((positions[:, None] >= prompt_ends[None, :]).astype(jnp.int32), axis=1)
    opens_prompt = (positions[0] == 0) | jnp.any(positions[0] == prompt_ends)
    through = jnp.logical_not(opens_prompt) & jnp.all(segment == segment[0])
    factor = jnp.where(through, jnp.exp(cumulative[-1]), 0.0)
    entry_seg = jnp.where(opens_prompt, -1, segment[0])
    empty_state = jnp.zeros((heads_here, head_width, head_width), jnp.float32)
    attention, end_state = attend(
        own_q, own_k, own_v, cumulative, segment, empty_state, jnp.int32(-1)
    )
    incoming = carried_state(factor, end_state)
    reach_back = jnp.where((segment == entry_seg)[:, None], jnp.exp(cumulative), 0.0)
    attention = (
        attention + paired_einsum("thd,hde->the", incoming, own_q, False) * reach_back[:, :, None]
    )
    inv_scale = lax.rsqrt(jnp.mean(attention * attention, axis=-1, keepdims=True) + 1e-06)
    normed = (attention * inv_scale * norm_gain.reshape(heads_here, head_width)).astype(
        jnp.bfloat16
    )
    normed = normed.reshape(row_count, heads_here * head_width)
    projected = jnp.dot(
        lax.all_gather(normed, "head", axis=1, tiled=True),
        out_weight,
        preferred_element_type=jnp.float32,
    )
    return projected.astype(jnp.bfloat16)


MESH = pl.DeviceIdType.MESH
NT = (((1,), (1,)), ((), ()))
TN = (((0,), (0,)), ((), ()))
STRIPE = 32


def dot32(left, right, dims=(((1,), (0,)), ((), ()))):
    return lax.dot_general(left, right, dims, preferred_element_type=jnp.float32)


def state_kernel(
    owners,
    rows,
    heads,
    lanes,
    slots,
    prompts,
    lengths_ref,
    pos_ref,
    decay_ref,
    gain_ref,
    q_ref,
    k_ref,
    v_ref,
    w_ref,
    out_ref,
    all_pos,
    all_decay,
    raw_in,
    ordered,
    sort_hot,
    place_hot,
    mask_bias,
    cum_col,
    cum_row,
    toward_col,
    reach_col,
    first_row,
    last_row,
    factor,
    states,
    merged,
    merged_in,
    prefix,
    normed,
    arrived,
    gathered,
    weights,
    total,
    meta_l,
    meta_s,
    meta_r,
    in_l,
    w_l,
    raw_s,
    raw_r,
    merged_s,
    merged_r,
    out_l,
    out_s,
    out_r,
    sib_s,
    sib_r,
    cross_s,
    cross_r,
    relay_s,
    relay_r,
):
    me = lax.axis_index("ctx")
    my_head = lax.axis_index("head")
    sibling = my_head + 1 - 2 * lax.rem(my_head, 2)
    cross = lax.rem(my_head + 2, 4)
    diagonal = lax.rem(sibling + 2, 4)
    tokens = owners * rows
    pairs = heads // 2
    wide = 2 * lanes
    peers = [lax.rem(me + step, owners) for step in (2, 1, 3)]
    far = jnp.where(me < 2, 2, 1)
    near = 3 - far
    edge = jnp.where(me < 2, 0, 3)
    inner = jnp.logical_or(me == 1, me == 2)
    outer = jnp.logical_not(inner)
    sources = (q_ref, k_ref, v_ref)

    def pair_block(index):
        return pl.ds(pl.multiple_of(index * wide, wide), wide)

    def lane_block(index):
        return pl.ds(pl.multiple_of(index * lanes, lanes), lanes)

    def token_block(index):
        return pl.ds(pl.multiple_of(index * rows, rows), rows)

    def in_local(a, p):
        return pltpu.make_async_copy(
            sources[a].at[:, pair_block(p)], raw_in.at[a, p], in_l.at[a, p]
        )

    def weight_load(h):
        return pltpu.make_async_copy(w_ref.at[:, h], weights.at[h], w_l.at[h])

    for p in range(pairs):
        for a in range(3):
            in_local(a, p).start()

    barrier = pltpu.get_barrier_semaphore()
    for peer in peers:
        pl.semaphore_signal(barrier, inc=1, device_id={"ctx": peer}, device_id_type=MESH)
    for peer in (sibling, cross):
        pl.semaphore_signal(barrier, inc=1, device_id={"head": peer}, device_id_type=MESH)

    def remote(source, target, send, recv, axis, device):
        return pltpu.make_async_remote_copy(
            src_ref=source,
            dst_ref=target,
            send_sem=send,
            recv_sem=recv,
            device_id={axis: device},
            device_id_type=MESH,
        )

    def pos_send(peer, source):
        return remote(
            pos_ref,
            all_pos.at[:, token_block(source)],
            meta_s.at[0, peer],
            meta_r.at[0, source],
            "ctx",
            peer,
        )

    def decay_send(peer, source):
        return remote(
            decay_ref,
            all_decay.at[:, token_block(source)],
            meta_s.at[1, peer],
            meta_r.at[1, source],
            "ctx",
            peer,
        )

    def raw_send(h, slot, peer, source):
        return remote(
            states.at[source, h],
            states.at[source, h],
            raw_s.at[slot, h],
            raw_r.at[source, h],
            "ctx",
            peer,
        )

    def merged_send(h):
        return remote(
            merged.at[h], merged_in.at[h], merged_s.at[h], merged_r.at[h], "ctx", edge
        )

    def out_send(h, owner, source):
        return remote(
            normed.at[h, owner],
            arrived.at[h, source],
            out_s.at[owner, h],
            out_r.at[source, h],
            "ctx",
            owner,
        )

    def out_local(h):
        return pltpu.make_async_copy(normed.at[h, me], arrived.at[h, me], out_l.at[h])

    def head_send(h, head_index, target, send, recv):
        piece = gathered.at[h, :, lane_block(head_index)]
        return remote(piece, piece, send.at[h], recv.at[h], "head", target)

    pos_local = pltpu.make_async_copy(pos_ref, all_pos.at[:, token_block(me)], meta_l.at[0])
    decay_local = pltpu.make_async_copy(
        decay_ref, all_decay.at[:, token_block(me)], meta_l.at[1]
    )
    pos_local.start()
    decay_local.start()
    for h in range(heads):
        weight_load(h).start()

    ends = []
    running = lengths_ref[0]
    for index in range(1, prompts):
        ends.append(running)
        running = running + lengths_ref[index]

    def segment_of(position):
        found = jnp.zeros_like(position)
        for end in ends:
            found = found + jnp.where(position >= end, 1, 0)
        return found

    own_pos = pos_ref[...].astype(jnp.float32)
    decay = decay_ref[...]
    slot_col = lax.broadcasted_iota(jnp.int32, (slots, 1), 0)
    slot_row = lax.broadcasted_iota(jnp.int32, (1, slots), 1)
    later = lax.broadcasted_iota(jnp.int32, (slots, slots), 0)
    sooner = lax.broadcasted_iota(jnp.int32, (slots, slots), 1)
    causal = later >= sooner
    lower = jnp.where(causal, 1.0, 0.0).astype(jnp.bfloat16)
    for o in range(owners):
        inside = (own_pos >= o * rows) & (own_pos < (o + 1) * rows)
        first = jnp.min(jnp.where(inside, own_pos, 1.0 * tokens), axis=1, keepdims=True)
        last = jnp.max(jnp.where(inside, own_pos, -1.0), axis=1, keepdims=True)
        first_at = first.astype(jnp.int32)
        last_at = last.astype(jnp.int32)
        here_col = first_at + slot_col
        here_row = first_at + slot_row
        wanted = jnp.where(here_col <= last_at, here_col, -1).astype(jnp.float32)
        hits = jnp.where(own_pos == wanted, 1.0, 0.0).astype(jnp.bfloat16)
        sort_hot[pl.ds(o * slots, slots), :] = hits
        decay_rows = dot32(decay, hits, NT).astype(jnp.bfloat16)
        decay_cols = dot32(hits, decay, NT).astype(jnp.bfloat16)
        row_sums = dot32(decay_rows, lower, NT)
        col_sums = dot32(lower, decay_cols)
        cum_row[o] = row_sums
        seg_col = segment_of(here_col)
        seg_row = segment_of(here_row)
        seg_first = segment_of(first_at)
        seg_last = segment_of(last_at)
        mask_bias[o] = jnp.where(causal & (seg_col == seg_row), 0.0, -1e30)
        toward = jnp.where(
            seg_col == seg_last, jnp.exp(col_sums[slots - 1 :, :] - col_sums), 0.0
        )
        reach = jnp.where(seg_col == seg_first, jnp.exp(col_sums), 0.0)
        for p in range(pairs):
            cum_col[p, o] = col_sums[:, 2 * p : 2 * p + 2]
            toward_col[p, o] = toward[:, 2 * p : 2 * p + 2]
            reach_col[p, o] = reach[:, 2 * p : 2 * p + 2]

    pl.semaphore_wait(barrier, owners + 1)
    for peer in peers:
        pos_send(peer, me).start()
        decay_send(peer, me).start()

    half = owners * slots // 2

    def make_states(p, carry):
        for a in range(3):
            in_local(a, p).wait()
            for part in range(2):
                block = pl.ds(part * half, half)
                ordered[a, p, block, :] = dot32(sort_hot[block, :], raw_in[a, p]).astype(
                    jnp.bfloat16
                )
        for j in range(2):
            h = 2 * p + j
            for o in range(owners):
                run = pl.ds(o * slots, slots)
                side = slice(j * lanes, (j + 1) * lanes)
                key = ordered[1, p, run, side]
                value = ordered[2, p, run, side]
                weighted = key.astype(jnp.float32) * toward_col[p, o][:, j : j + 1]
                states[me, h, o] = dot32(weighted.astype(jnp.bfloat16), value, TN).astype(
                    jnp.bfloat16
                )
            raw_send(h, 0, far, me).start()

            @pl.when(outer)
            def _():
                raw_send(h, 1, near, me).start()

        return carry

    lax.fori_loop(0, pairs, make_states, 0)

    pos_local.wait()
    decay_local.wait()
    for peer in peers:
        pos_send(me, peer).wait_recv()
        decay_send(me, peer).wait_recv()

    group_iota = lax.broadcasted_iota(jnp.int32, (8, rows), 0).astype(jnp.float32) * rows
    for d in range(owners):
        held = all_pos[:, d * rows : (d + 1) * rows].astype(jnp.float32)
        inside = (held >= group_iota) & (held < group_iota + rows)
        first = jnp.min(jnp.where(inside, held, 1.0 * tokens), axis=1, keepdims=True)
        last = jnp.max(jnp.where(inside, held, -1.0), axis=1, keepdims=True)
        first_row[d * 8 : d * 8 + 8, :] = jnp.broadcast_to(first, (8, lanes))
        last_row[d * 8 : d * 8 + 8, :] = jnp.broadcast_to(last, (8, lanes))

    every_pos = all_pos[...].astype(jnp.float32)
    every_decay = all_decay[...]
    last_all = last_row[...][:, :1]
    seg_all = segment_of(last_all.astype(jnp.int32))
    holder = lax.broadcasted_iota(jnp.int32, (8 * owners, 1), 0) // 8
    for t in range(2 * owners):
        device = me if t < owners else edge
        start = first_row[pl.ds(device * 8 + t % owners, 1), :][:, :1]
        between = (every_pos > last_all) & (every_pos < start)
        sums = dot32(jnp.where(between, 1.0, 0.0).astype(jnp.bfloat16), every_decay, NT)
        linked = (last_all < start) & (seg_all == segment_of(start.astype(jnp.int32)))
        if t >= owners:
            linked = linked & (holder != edge)
        scale = jnp.where(linked, jnp.exp(sums), 0.0)
        for h in range(heads):
            factor[h, t] = jnp.broadcast_to(scale[:, h : h + 1], (8 * owners, lanes))

    line = lax.broadcasted_iota(jnp.int32, (1, owners * slots), 1).astype(jnp.float32)
    source_pos = jnp.full((1, owners * slots), -1.0, jnp.float32)
    for d in range(owners):
        first = first_row[pl.ds(d * 8 + me, 1), :][:, :1]
        last = last_row[pl.ds(d * 8 + me, 1), :][:, :1]
        found = first + (line - 1.0 * d * slots)
        fine = (line >= d * slots) & (line < (d + 1) * slots) & (found <= last)
        source_pos = jnp.where(fine, found, source_pos)
    target_pos = (me * rows + lax.broadcasted_iota(jnp.int32, (rows, 1), 0)).astype(jnp.float32)
    place_hot[...] = jnp.where(target_pos == source_pos, 1.0, 0.0).astype(jnp.bfloat16)
    total[...] = jnp.zeros_like(total)

    def stripe(index):
        return pl.ds(pl.multiple_of(index * STRIPE, STRIPE), STRIPE)

    def merge_inner(h):
        def body(index, carry):
            block = stripe(index)
            sums = [None] * (2 * owners)
            for d in range(owners):
                for past in range(owners):
                    tile = states[d, h, past, block, :].astype(jnp.float32)
                    for t in range(2 * owners):
                        if past <= t % owners:
                            term = tile * factor[h, t, pl.ds(d * 8 + past, 1), :]
                            sums[t] = term if sums[t] is None else sums[t] + term
            for o in range(owners):
                prefix[o, block, :] = sums[o].astype(jnp.bfloat16)
                merged[h, o, block, :] = sums[owners + o].astype(jnp.bfloat16)
            return carry

        lax.fori_loop(0, lanes // STRIPE, body, 0)

    def merge_outer(h):
        def body(index, carry):
            block = stripe(index)
            for o in range(owners):
                summed = merged_in[h, o, block, :].astype(jnp.float32)
                for past in range(o):
                    tile = states[me, h, past, block, :].astype(jnp.float32)
                    summed = summed + tile * factor[h, o, pl.ds(me * 8 + past, 1), :]
                prefix[o, block, :] = summed.astype(jnp.bfloat16)
            return carry

        lax.fori_loop(0, lanes // STRIPE, body, 0)

    def attend_pair(p, carry):
        for j in range(2):
            h = 2 * p + j

            @pl.when(inner)
            def _():
                for peer in peers:
                    raw_send(h, 0, me, peer).wait_recv()
                merge_inner(h)
                merged_send(h).start()

            @pl.when(outer)
            def _():
                merged_send(h).wait_recv()
                merge_outer(h)

            gain = gain_ref[pl.ds(h, 1), :]
            for o in range(owners):
                run = pl.ds(o * slots, slots)
                side = slice(j * lanes, (j + 1) * lanes)
                query = ordered[0, p, run, side]
                key = ordered[1, p, run, side]
                value = ordered[2, p, run, side]
                col = cum_col[p, o][:, j : j + 1]
                row = cum_row[o, pl.ds(h, 1), :]
                table = jnp.exp(col - row + mask_bias[o])
                scores = (dot32(query, key, NT) * table).astype(jnp.bfloat16)
                result = dot32(scores, value)
                result = result + dot32(query, prefix[o]) * reach_col[p, o][:, j : j + 1]
                scale = lax.rsqrt(jnp.mean(result * result, axis=-1, keepdims=True) + 1e-06)
                normed[h, o] = (result * scale * gain).astype(jnp.bfloat16)
            for peer in peers:
                out_send(h, peer, me).start()
            out_local(h).start()
        return carry

    lax.fori_loop(0, pairs, attend_pair, 0)

    def place(h):
        out_local(h).wait()
        for peer in peers:
            out_send(h, me, peer).wait_recv()
        incoming = arrived[h].reshape(owners * slots, lanes)
        gathered[h, :, lane_block(my_head)] = dot32(place_hot[...], incoming).astype(
            jnp.bfloat16
        )
        head_send(h, my_head, cross, cross_s, cross_r).start()
        head_send(h, my_head, sibling, sib_s, sib_r).start()

    def relay(h):
        head_send(h, cross, cross, cross_s, cross_r).wait_recv()
        head_send(h, cross, sibling, relay_s, relay_r).start()

    width = out_ref.shape[1]
    tile = 256

    def project(h, final):
        head_send(h, sibling, sibling, sib_s, sib_r).wait_recv()
        head_send(h, diagonal, sibling, relay_s, relay_r).wait_recv()

        def columns_of(index, carry):
            columns = pl.ds(pl.multiple_of(index * tile, tile), tile)
            right = weights[h, :, :, columns].reshape(4 * lanes, tile)
            summed = total[:, columns] + dot32(gathered[h], right)
            if final:
                out_ref[:, columns] = summed.astype(out_ref.dtype)
            else:
                total[:, columns] = summed
            return carry

        lax.fori_loop(0, width // tile, columns_of, 0)

    for h in range(heads):
        weight_load(h).wait()

    def finish_pair(p, carry):
        @pl.when(p > 0)
        def _():
            relay(2 * p - 1)

        place(2 * p)

        @pl.when(p > 0)
        def _():
            project(2 * p - 1, False)

        relay(2 * p)
        place(2 * p + 1)
        project(2 * p, False)
        return carry

    lax.fori_loop(0, pairs, finish_pair, 0)
    relay(heads - 1)
    project(heads - 1, True)

    for peer in peers:
        pos_send(peer, me).wait_send()
        decay_send(peer, me).wait_send()

    def drain(h, carry):
        raw_send(h, 0, far, me).wait_send()

        @pl.when(outer)
        def _():
            raw_send(h, 1, near, me).wait_send()

        @pl.when(inner)
        def _():
            merged_send(h).wait_send()

        for peer in peers:
            out_send(h, peer, me).wait_send()
        head_send(h, my_head, cross, cross_s, cross_r).wait_send()
        head_send(h, my_head, sibling, sib_s, sib_r).wait_send()
        head_send(h, cross, sibling, relay_s, relay_r).wait_send()
        return carry

    lax.fori_loop(0, heads, drain, 0)


def fused_form(
    queries, keys, values, log_decay, arrival_positions, prompt_lengths, norm_gain, out_weight
):
    rows = queries.shape[0]
    heads = log_decay.shape[1]
    lanes = queries.shape[1] // heads
    owners = lax.axis_size("ctx")
    columns = lax.axis_size("head")
    tokens = owners * rows
    slots = 3 * (rows // (2 * owners))
    pairs = heads // 2
    wide = 2 * lanes
    padded = owners * slots
    features, width = out_weight.shape
    gain = norm_gain.reshape(heads, lanes)
    stacked = out_weight.reshape(columns, heads, lanes, width)
    vmem = pl.BlockSpec(memory_space=pltpu.VMEM)
    anywhere = pl.BlockSpec(memory_space=pl.ANY)
    dma = pltpu.SemaphoreType.DMA
    bf16, f32 = jnp.bfloat16, jnp.float32
    return pl.pallas_call(
        functools.partial(
            state_kernel, owners, rows, heads, lanes, slots, prompt_lengths.shape[0]
        ),
        out_shape=jax.ShapeDtypeStruct((rows, width), bf16),
        in_specs=[
            pl.BlockSpec(memory_space=pltpu.SMEM),
            vmem,
            vmem,
            vmem,
            anywhere,
            anywhere,
            anywhere,
            anywhere,
        ],
        out_specs=vmem,
        scratch_shapes=[
            pltpu.VMEM((1, tokens), jnp.int32),
            pltpu.VMEM((heads, tokens), bf16),
            pltpu.VMEM((3, pairs, rows, wide), bf16),
            pltpu.VMEM((3, pairs, padded, wide), bf16),
            pltpu.VMEM((padded, rows), bf16),
            pltpu.VMEM((rows, padded), bf16),
            pltpu.VMEM((owners, slots, slots), f32),
            pltpu.VMEM((pairs, owners, slots, 2), f32),
            pltpu.VMEM((owners, heads, slots), f32),
            pltpu.VMEM((pairs, owners, slots, 2), f32),
            pltpu.VMEM((pairs, owners, slots, 2), f32),
            pltpu.VMEM((8 * owners, lanes), f32),
            pltpu.VMEM((8 * owners, lanes), f32),
            pltpu.VMEM((heads, 2 * owners, 8 * owners, lanes), f32),
            pltpu.VMEM((owners, heads, owners, lanes, lanes), bf16),
            pltpu.VMEM((heads, owners, lanes, lanes), bf16),
            pltpu.VMEM((heads, owners, lanes, lanes), bf16),
            pltpu.VMEM((owners, lanes, lanes), bf16),
            pltpu.VMEM((heads, owners, slots, lanes), bf16),
            pltpu.VMEM((heads, owners, slots, lanes), bf16),
            pltpu.VMEM((heads, rows, columns * lanes), bf16),
            pltpu.VMEM((heads, columns, lanes, width), bf16),
            pltpu.VMEM((rows, width), f32),
            dma((2,)),
            dma((2, owners)),
            dma((2, owners)),
            dma((3, pairs)),
            dma((heads,)),
            dma((2, heads)),
            dma((owners, heads)),
            dma((heads,)),
            dma((heads,)),
            dma((heads,)),
            dma((owners, heads)),
            dma((owners, heads)),
            dma((heads,)),
            dma((heads,)),
            dma((heads,)),
            dma((heads,)),
            dma((heads,)),
            dma((heads,)),
        ],
        compiler_params=pltpu.CompilerParams(
            collective_id=0, has_side_effects=True, vmem_limit_bytes=58 * 1024 * 1024
        ),
    )(
        prompt_lengths,
        arrival_positions.reshape(1, rows),
        log_decay.T,
        gain,
        queries,
        keys,
        values,
        stacked,
    )


def local(*arguments):
    queries, log_decay = arguments[0], arguments[3]
    fits = (
        log_decay.shape[1] == 8
        and lax.axis_size("ctx") == 4
        and lax.axis_size("head") == 4
        and queries.shape[0] == 512
        and queries.shape[1] == 128 * log_decay.shape[1]
    )
    return (fused_form if fits else exchange_form)(*arguments)


def solution(mesh):
    return jax.shard_map(
        local,
        mesh=mesh,
        in_specs=(
            P(("groups", "ctx"), "head"),
            P(("groups", "ctx"), "head"),
            P(("groups", "ctx"), "head"),
            P(("groups", "ctx"), "head"),
            P(("groups", "ctx")),
            P("groups"),
            P("head"),
            P(None, "head"),
        ),
        out_specs=P(("groups", "ctx"), "head"),
        check_vma=False,
    )
```

time: 121 us -> 110 us (0.909); the launches traced: 121 us -> 108 us
  Pallas kernels: 116 us -> 105 us
  other arithmetic: 2.09 us -> 0 us
    pallas_call x1, Pallas kernels: 116 us -> 105 us  [fused_form(): pl.pallas_call(functools.partial(state_kernel, owners, rows, heads, lanes...]
where the time goes in v1:
time: 110 us; the launch traced here: 108 us
  Pallas kernels  105 us (95%)
  local copies, waits for them, and re-layouts  2.65 us (2%)
    pallas_call x1, Pallas kernels, fused_form(): pl.pallas_call(functools.partial(state_kernel, owners, rows, heads, lanes...  105 us
    unnamed x1, local copies, waits for them, and re-layouts  2.65 us

profile of v1, /device:TPU:8, one launch (start us, length us, event | category | flops | bytes accessed | tf_op | source)
XLA Modules:
  0.0 108.1 jit_solution(7783976761255907489)
XLA Ops:
  0.0 105.5 %shard_map.82 = bf16[512,1536]{1,0:T(8,128)(2,1)} custom-call(s32[4]{0:T(128)} %lengths_ref.1, s32[1,512]{1,0:T(1,128)} %bitcast.7, bf16[8,512]{1,0:T(8,128)(2,1)} %bitcast.5, f32[8,128]{1,0:T(8,128)} %bitcast.6, bf16[512,1024]{1,0:T(8,128)(2,1)} %q_ref.1, bf16[512,1024]{1,0:T(8,128)(2,1)} %k_ref.1, bf16[512,1024]{1,0:T(8,128)(2,1)} %v_ref.1, ...), custom_call_target="tpu_custom_call" | custom-call | tf_op jit(solution)/shard_map/pallas_call | solution.py:640
  105.5 2.7 %copy.10 = bf16[512,1536]{1,0:T(8,128)(2,1)} copy(bf16[512,1536]{1,0:T(8,128)(2,1)} %shard_map.82) | data formatting | bytes 3145728

commit v2 on v1

--- a/solution.py
+++ b/solution.py
@@ -253,8 +253,10 @@
         return pltpu.make_async_copy(w_ref.at[:, h], weights.at[h], w_l.at[h])
 
     for p in range(pairs):
-        for a in range(3):
+        for a in (1, 2):
             in_local(a, p).start()
+    for p in range(pairs):
+        in_local(0, p).start()
 
     barrier = pltpu.get_barrier_semaphore()
     for peer in peers:
@@ -353,35 +355,28 @@
     sooner = lax.broadcasted_iota(jnp.int32, (slots, slots), 1)
     causal = later >= sooner
     lower = jnp.where(causal, 1.0, 0.0).astype(jnp.bfloat16)
+    bounds = []
     for o in range(owners):
         inside = (own_pos >= o * rows) & (own_pos < (o + 1) * rows)
         first = jnp.min(jnp.where(inside, own_pos, 1.0 * tokens), axis=1, keepdims=True)
         last = jnp.max(jnp.where(inside, own_pos, -1.0), axis=1, keepdims=True)
         first_at = first.astype(jnp.int32)
         last_at = last.astype(jnp.int32)
+        bounds.append((first_at, last_at))
         here_col = first_at + slot_col
-        here_row = first_at + slot_row
         wanted = jnp.where(here_col <= last_at, here_col, -1).astype(jnp.float32)
         hits = jnp.where(own_pos == wanted, 1.0, 0.0).astype(jnp.bfloat16)
         sort_hot[pl.ds(o * slots, slots), :] = hits
-        decay_rows = dot32(decay, hits, NT).astype(jnp.bfloat16)
         decay_cols = dot32(hits, decay, NT).astype(jnp.bfloat16)
-        row_sums = dot32(decay_rows, lower, NT)
         col_sums = dot32(lower, decay_cols)
-        cum_row[o] = row_sums
-        seg_col = segment_of(here_col)
-        seg_row = segment_of(here_row)
-        seg_first = segment_of(first_at)
-        seg_last = segment_of(last_at)
-        mask_bias[o] = jnp.where(causal & (seg_col == seg_row), 0.0, -1e30)
         toward = jnp.where(
-            seg_col == seg_last, jnp.exp(col_sums[slots - 1 :, :] - col_sums), 0.0
-        )
-        reach = jnp.where(seg_col == seg_first, jnp.exp(col_sums), 0.0)
+            segment_of(here_col) == segment_of(last_at),
+            jnp.exp(col_sums[slots - 1 :, :] - col_sums),
+            0.0,
+        )
         for p in range(pairs):
             cum_col[p, o] = col_sums[:, 2 * p : 2 * p + 2]
             toward_col[p, o] = toward[:, 2 * p : 2 * p + 2]
-            reach_col[p, o] = reach[:, 2 * p : 2 * p + 2]
 
     pl.semaphore_wait(barrier, owners + 1)
     for peer in peers:
@@ -390,14 +385,17 @@
 
     half = owners * slots // 2
 
+    def sort_rows(a, p):
+        in_local(a, p).wait()
+        for part in range(2):
+            block = pl.ds(part * half, half)
+            ordered[a, p, block, :] = dot32(sort_hot[block, :], raw_in[a, p]).astype(
+                jnp.bfloat16
+            )
+
     def make_states(p, carry):
-        for a in range(3):
-            in_local(a, p).wait()
-            for part in range(2):
-                block = pl.ds(part * half, half)
-                ordered[a, p, block, :] = dot32(sort_hot[block, :], raw_in[a, p]).astype(
-                    jnp.bfloat16
-                )
+        sort_rows(1, p)
+        sort_rows(2, p)
         for j in range(2):
             h = 2 * p + j
             for o in range(owners):
@@ -418,6 +416,24 @@
         return carry
 
     lax.fori_loop(0, pairs, make_states, 0)
+
+    for o in range(owners):
+        first_at, last_at = bounds[o]
+        hits = sort_hot[pl.ds(o * slots, slots), :]
+        decay_rows = dot32(decay, hits, NT).astype(jnp.bfloat16)
+        cum_row[o] = dot32(decay_rows, lower, NT)
+        seg_col = segment_of(first_at + slot_col)
+        seg_row = segment_of(first_at + slot_row)
+        seg_first = segment_of(first_at)
+        mask_bias[o] = jnp.where(causal & (seg_col == seg_row), 0.0, -1e30)
+        for p in range(pairs):
+            reach_col[p, o] = jnp.where(seg_col == seg_first, jnp.exp(cum_col[p, o]), 0.0)
+
+    def sort_queries(p, carry):
+        sort_rows(0, p)
+        return carry
+
+    lax.fori_loop(0, pairs, sort_queries, 0)
 
     pos_local.wait()
     decay_local.wait()
@@ -572,24 +588,22 @@
     for h in range(heads):
         weight_load(h).wait()
 
+    place(0)
+    place(1)
+    relay(0)
+
     def finish_pair(p, carry):
-        @pl.when(p > 0)
-        def _():
-            relay(2 * p - 1)
-
         place(2 * p)
-
-        @pl.when(p > 0)
-        def _():
-            project(2 * p - 1, False)
-
+        relay(2 * p - 1)
+        project(2 * p - 2, False)
+        place(2 * p + 1)
         relay(2 * p)
-        place(2 * p + 1)
-        project(2 * p, False)
+        project(2 * p - 1, False)
         return carry
 
-    lax.fori_loop(0, pairs, finish_pair, 0)
+    lax.fori_loop(1, pairs, finish_pair, 0)
     relay(heads - 1)
+    project(heads - 2, False)
     project(heads - 1, True)
 
     for peer in peers:

time: 110 us -> 106 us (0.964); the launches traced: 108 us -> 106 us
  Pallas kernels: 105 us -> 103 us
    pallas_call x1, Pallas kernels: 105 us -> 103 us  [fused_form(): pl.pallas_call(functools.partial(state_kernel, owners, rows, heads, lanes...]
where the time goes in v2:
time: 106 us
  Pallas kernels  103 us (97%)
  local copies, waits for them, and re-layouts  2.65 us (2%)
    pallas_call x1, Pallas kernels, fused_form(): pl.pallas_call(functools.partial(state_kernel, owners, rows, heads, lanes...  103 us
    unnamed x1, local copies, waits for them, and re-layouts  2.65 us

profile of v2, /device:TPU:8, one launch (start us, length us, event | category | flops | bytes accessed | tf_op | source)
XLA Modules:
  0.0 105.7 jit_solution(3841823971080228955)
XLA Ops:
  0.0 103.1 %shard_map.82 = bf16[512,1536]{1,0:T(8,128)(2,1)} custom-call(s32[4]{0:T(128)} %lengths_ref.1, s32[1,512]{1,0:T(1,128)} %bitcast.7, bf16[8,512]{1,0:T(8,128)(2,1)} %bitcast.5, f32[8,128]{1,0:T(8,128)} %bitcast.6, bf16[512,1024]{1,0:T(8,128)(2,1)} %q_ref.1, bf16[512,1024]{1,0:T(8,128)(2,1)} %k_ref.1, bf16[512,1024]{1,0:T(8,128)(2,1)} %v_ref.1, ...), custom_call_target="tpu_custom_call" | custom-call | tf_op jit(solution)/shard_map/pallas_call | solution.py:654
  103.1 2.7 %copy.10 = bf16[512,1536]{1,0:T(8,128)(2,1)} copy(bf16[512,1536]{1,0:T(8,128)(2,1)} %shard_map.82) | data formatting | bytes 3145728

commit v3 on v2

--- a/solution.py
+++ b/solution.py
@@ -218,6 +218,8 @@
     cross_r,
     relay_s,
     relay_r,
+    result,
+    result_s,
 ):
     me = lax.axis_index("ctx")
     my_head = lax.axis_index("head")
@@ -227,7 +229,12 @@
     tokens = owners * rows
     pairs = heads // 2
     wide = 2 * lanes
-    peers = [lax.rem(me + step, owners) for step in (2, 1, 3)]
+    left_side = me < 2
+    peers = [
+        jnp.where(left_side, 3, 0),
+        jnp.where(left_side, 2, 1),
+        me + 1 - 2 * lax.rem(me, 2),
+    ]
     far = jnp.where(me < 2, 2, 1)
     near = 3 - far
     edge = jnp.where(me < 2, 0, 3)
@@ -567,7 +574,13 @@
         head_send(h, cross, sibling, relay_s, relay_r).start()
 
     width = out_ref.shape[1]
-    tile = 256
+    tile = 768
+
+    def store(index):
+        columns = pl.ds(pl.multiple_of(index * tile, tile), tile)
+        return pltpu.make_async_copy(
+            result.at[:, columns], out_ref.at[:, columns], result_s.at[index]
+        )
 
     def project(h, final):
         head_send(h, sibling, sibling, sib_s, sib_r).wait_recv()
@@ -578,7 +591,8 @@
             right = weights[h, :, :, columns].reshape(4 * lanes, tile)
             summed = total[:, columns] + dot32(gathered[h], right)
             if final:
-                out_ref[:, columns] = summed.astype(out_ref.dtype)
+                result[:, columns] = summed.astype(out_ref.dtype)
+                store(index).start()
             else:
                 total[:, columns] = summed
             return carry
@@ -629,6 +643,8 @@
         return carry
 
     lax.fori_loop(0, heads, drain, 0)
+    for index in range(width // tile):
+        store(index).wait()
 
 
 def fused_form(
@@ -666,7 +682,7 @@
             anywhere,
             anywhere,
         ],
-        out_specs=vmem,
+        out_specs=anywhere,
         scratch_shapes=[
             pltpu.VMEM((1, tokens), jnp.int32),
             pltpu.VMEM((heads, tokens), bf16),
@@ -709,6 +725,8 @@
             dma((heads,)),
             dma((heads,)),
             dma((heads,)),
+            pltpu.VMEM((rows, width), bf16),
+            dma((width // 768,)),
         ],
         compiler_params=pltpu.CompilerParams(
             collective_id=0, has_side_effects=True, vmem_limit_bytes=58 * 1024 * 1024

time: 106 us -> 103 us (0.972)
  Pallas kernels: 103 us -> 100 us
    pallas_call x1, Pallas kernels: 103 us -> 100 us  [fused_form(): pl.pallas_call(functools.partial(state_kernel, owners, rows, heads, lanes...]
where the time goes in v3:
time: 103 us
  Pallas kernels  100 us (97%)
  local copies, waits for them, and re-layouts  2.65 us (3%)
    pallas_call x1, Pallas kernels, fused_form(): pl.pallas_call(functools.partial(state_kernel, owners, rows, heads, lanes...  100 us
    unnamed x1, local copies, waits for them, and re-layouts  2.65 us

profile of v3, /device:TPU:8, one launch (start us, length us, event | category | flops | bytes accessed | tf_op | source)
XLA Modules:
  0.0 102.7 jit_solution(5185946124394957636)
XLA Ops:
  0.0 100.0 %shard_map.82 = bf16[512,1536]{1,0:T(8,128)(2,1)} custom-call(s32[4]{0:T(128)} %lengths_ref.1, s32[1,512]{1,0:T(1,128)} %bitcast.7, bf16[8,512]{1,0:T(8,128)(2,1)} %bitcast.5, f32[8,128]{1,0:T(8,128)} %bitcast.6, bf16[512,1024]{1,0:T(8,128)(2,1)} %q_ref.1, bf16[512,1024]{1,0:T(8,128)(2,1)} %k_ref.1, bf16[512,1024]{1,0:T(8,128)(2,1)} %v_ref.1, ...), custom_call_target="tpu_custom_call" | custom-call | tf_op jit(solution)/shard_map/pallas_call | solution.py:670
  100.0 2.7 %copy.10 = bf16[512,1536]{1,0:T(8,128)(2,1)} copy(bf16[512,1536]{1,0:T(8,128)(2,1)} %shard_map.82) | data formatting | bytes 3145728
